TPU v7x, 1024 devices: a whole 4x4x32 slice. The times are simulated.
1024 devices in a mesh: graph: 256 (over z, y, core), group: 4 (over x).
Axes of the slice: x: 4, y: 4, z: 32, core: 2. Of those that a mesh axis runs over, the one named last changes fastest.
Arguments:
- state: bfloat16 [14, 1048576], P(None, 'graph'), may hold values from -6 to 6
- cotangent: float32 [4, 14, 1048576], P('group', None, 'graph'), may hold values from -6 to 6
- diffusivity: float32 [3, 2048], P(None, 'graph'), may hold values from 0.0001 to 0.001
- shared_nodes: int32 [256, 8, 384], P('graph'), may hold values from -1 to 4095, as said below
- w_in: bfloat16 [14, 128], replicated, may hold values from -1.5 to 1.5
- b_in: float32 [128], replicated, may hold values from -3 to 3
- w_mid: bfloat16 [128, 128], replicated, may hold values from -0.5 to 0.5
- b_mid: float32 [128], replicated, may hold values from -3 to 3
- w_out: bfloat16 [128, 14], replicated, may hold values from -0.5 to 0.5
Outputs:
- grad_state: float32 [4, 14, 1048576], P('group', None, 'graph')
- grad_w_in: float32 [14, 128], replicated
- grad_w_mid: float32 [128, 128], replicated
- grad_w_out: float32 [128, 14], replicated
Inputs may be any that keep to these rules, and one draw needn't show every extreme that they name: `shared_nodes`: each partition-local node stands in at most one list of its partition; the lists of directions that leave the grid of 4 x (64) partitions are empty; every other list holds its nodes in its leading slots, matching its partner list's count: 192 to 384 nodes for the four face directions (o = +-1, +-4), with some list holding 384, and 24 to 48 nodes for the four diagonal directions, with some list holding 384 / 8.
All inputs are finite; a program needn't handle non-finite values.
Results may differ from a plain program's by a relative error of at most 0.0077.
Values sent between devices are 32-bit elements; how exact they have to be, the bound alone decides.
A program may use at most 32 MiB of HBM per device.

v0:
```python
import jax
import jax.numpy as jnp
import numpy as np
from jax import lax
from jax.sharding import PartitionSpec as P

NODES = 512
PROWS = 4


step_scale = 0.5


def from_behind(block, axis, distance):
    devices = range(lax.axis_size(axis))
    route = [(i - distance, i) for i in devices if i - distance in devices]
    return lax.ppermute(block, axis, route)


def stiffness_table():
    order = 7
    points = np.cos(np.pi * np.arange(order + 1) / order)
    ends = np.ones(order + 1)
    ends[0] = 2.0
    ends[-1] = 2.0
    deriv = np.zeros((order + 1, order + 1))
    for first in range(order + 1):
        for second in range(order + 1):
            if first != second:
                deriv[first, second] = (
                    ends[first]
                    / ends[second]
                    * (-1.0) ** (first + second)
                    / (points[first] - points[second])
                )
    row_sums = deriv.sum(axis=1)
    for place in range(order + 1):
        deriv[place, place] = -row_sums[place]
    return deriv.T @ deriv


def direction_tables():
    table = stiffness_table()
    eye_eight = np.eye(8)
    eye_wide = np.eye(64)
    along_one = np.kron(table, eye_wide)
    along_two = np.kron(eye_eight, np.kron(table, eye_eight))
    along_three = np.kron(eye_wide, table)
    return [
        jnp.asarray(matrix.T, dtype=jnp.float32) for matrix in (along_one, along_two, along_three)
    ]


def peer_offsets():
    return [1, -1, PROWS, -PROWS, PROWS + 1, -PROWS - 1, PROWS - 1, -PROWS + 1]


def diffuse(assembled, diffusivity, fields, elements):
    highest = lax.Precision.HIGHEST
    rows = assembled.reshape(fields * elements, NODES)
    total = jnp.zeros((fields, elements, NODES), jnp.float32)
    for which, matrix in enumerate(direction_tables()):
        applied = jnp.dot(rows, matrix, precision=highest).reshape(fields, elements, NODES)
        total = total + diffusivity[which][None, :, None] * applied
    return -total.reshape(fields, elements * NODES)


def per_device(state, cotangent, diffusivity, shared_nodes, w_in, b_in, w_mid, b_mid, w_out):
    fields, local = state.shape
    elements = local // NODES
    lists = shared_nodes[0]
    valid = (lists >= 0).astype(jnp.float32)
    safe = jnp.maximum(lists, 0)
    shared = jnp.zeros((local,), jnp.float32).at[safe.reshape(-1)].max(valid.reshape(-1))
    scaled = cotangent[0] / (1.0 + shared)[None, :]
    outgoing = [scaled[:, safe[which]] * valid[which][None, :] for which in range(8)]
    assembled = scaled
    for which, offset in enumerate(peer_offsets()):
        arrived = from_behind(outgoing[which], "graph", offset)
        deposit_which = which ^ 1
        assembled = assembled.at[:, safe[deposit_which]].add(
            arrived * valid[deposit_which][None, :]
        )
    viscous = diffuse(assembled, diffusivity, fields, elements)
    pre_first = (
        jnp.einsum("fp,fh->hp", state, w_in, preferred_element_type=jnp.float32) + b_in[:, None]
    )
    first = jnp.tanh(pre_first).astype(jnp.bfloat16)
    pre_second = (
        jnp.einsum("gp,gh->hp", first, w_mid, preferred_element_type=jnp.float32) + b_mid[:, None]
    )
    second = jnp.tanh(pre_second).astype(jnp.bfloat16)
    impulse = (step_scale * assembled).astype(jnp.bfloat16)
    second_wide = second.astype(jnp.float32)
    first_wide = first.astype(jnp.float32)
    back_second = jnp.einsum("hf,fp->hp", w_out, impulse, preferred_element_type=jnp.float32) * (
        1.0 - second_wide * second_wide
    )
    back_second = back_second.astype(jnp.bfloat16)
    back_first = jnp.einsum("gh,hp->gp", w_mid, back_second, preferred_element_type=jnp.float32) * (
        1.0 - first_wide * first_wide
    )
    back_first = back_first.astype(jnp.bfloat16)
    toward = jnp.einsum("fg,gp->fp", w_in, back_first, preferred_element_type=jnp.float32)
    grad_state = assembled + step_scale * viscous + toward
    grad_in = jnp.einsum("fp,gp->fg", state, back_first, preferred_element_type=jnp.float32)
    grad_mid = jnp.einsum("gp,hp->gh", first, back_second, preferred_element_type=jnp.float32)
    grad_out = jnp.einsum("hp,fp->hf", second, impulse, preferred_element_type=jnp.float32)
    summed = lax.psum((grad_in, grad_mid, grad_out), ("graph", "group"))
    return (grad_state[None], summed[0], summed[1], summed[2])


def solution(mesh):
    in_specs = (
        P(None, "graph"),
        P("group", None, "graph"),
        P(None, "graph"),
        P("graph", None, None),
        P(),
        P(),
        P(),
        P(),
        P(),
    )
    out_specs = (P("group", None, "graph"), P(), P(), P())
    return jax.shard_map(
        per_device, mesh=mesh, in_specs=in_specs, out_specs=out_specs, check_vma=False
    )
```

profile of v0, /device:TPU:1, one launch (start us, length us, event | category | flops | bytes accessed | tf_op | source)
XLA Modules:
  0.0 1018.2 jit_solution(18013144895227831625)
XLA Ops:
  7.2 0.7 broadcast_maximum_fusion
  8.9 20.2 %scatter_custom_fusion = f32[4096]{0:T(1024)S(1)} fusion(s32[3072]{0:T(1024)S(1)} %reshape.376, f32[3072]{0:T(1024)S(1)} %reshape.378, f32[]{:T(128)} %constant.8.clone.1), kind=kCustom, calls=%fused_computation.91 | custom fusion | flops 3072 | bytes 16388 | tf_op jit(solution)/shard_map/scatter-max | solution.py:74
  29.1 2.7 copy.23
  31.8 1.9 bitcast_divide_fusion
  33.8 1.1 gather_fusion
  34.9 0.8 multiply_bitcast_fusion.7
  35.7 4.5 collective-permute-start
  40.2 1.1 gather_fusion.1
  41.4 0.8 multiply_bitcast_fusion.6
  42.2 13.9 %collective-permute-start.1 = (f32[14,384]{0,1:T(8,128)}, f32[14,384]{0,1:T(8,128)}, u32[]{:S(2)}, u32[]{:S(2)}) collective-permute-start(f32[14,384]{0,1:T(8,128)} %multiply_bitcast_fusion.6), channel_id=1, source_target_pairs={{4,0},{8,4},{12,8},{16,12},{20,16},{24,20},{28,24},{32,28},{36,32}... | collective-permute-start | bytes 64520 | tf_op jit(solution)/shard_map/ppermute | solution.py:17
  56.2 1.1 gather_fusion.2
  57.3 0.8 multiply_bitcast_fusion.5
  58.1 2.0 collective-permute-start.2
  60.1 1.1 gather_fusion.3
  61.2 0.8 multiply_bitcast_fusion.4
  62.0 1.3 collective-permute-start.3
  63.3 1.1 gather_fusion.4
  64.5 0.8 multiply_bitcast_fusion.3
  65.2 2.0 collective-permute-start.4
  67.2 1.1 gather_fusion.5
  68.4 1.1 gather_fusion.6
  69.5 1.1 gather_fusion.7
  70.6 0.8 multiply_bitcast_fusion.2
  71.4 0.8 multiply_bitcast_fusion.1
  72.2 1.1 fusion.4
  73.3 2.2 fusion.5
  75.5 0.8 multiply_bitcast_fusion
  76.3 1.3 collective-permute-start.5
  77.6 5.7 collective-permute-start.6
  83.3 1.3 collective-permute-start.7
  85.2 3.9 scatter_custom_fusion.1
  89.2 4.1 scatter_custom_fusion.2
  93.3 4.5 scatter_custom_fusion.3
  97.8 4.3 scatter_custom_fusion.4
  102.1 4.5 scatter_custom_fusion.5
  106.7 4.4 scatter_custom_fusion.6
  111.1 4.5 scatter_custom_fusion.7
  115.6 4.3 scatter_custom_fusion.8
  120.5 1.7 fusion.7
  123.1 1.5 fusion.6
  124.5 1.1 fusion.59
  125.6 4.9 fusion.56
  130.5 3.5 fusion.57
  134.0 3.6 fusion.58
  138.9 0.9 copy.29
  139.9 169.5 %all-reduce = (f32[14,128]{1,0:T(8,128)}, f32[128,14]{0,1:T(8,128)}) all-reduce(f32[14,128]{1,0:T(8,128)S(1)} %convolution_bitcast_fusion.2, f32[128,14]{0,1:T(8,128)S(1)} %fusion.7), channel_id=1, replica_groups=mesh['graph'=256,'group'=4] {'graph','group'}, use_global_device_ids=true, to_apply=%region_9.0 | all-reduce | flops 3584 | bytes 28672 | tf_op jit(solution)/shard_map/psum | solution.py:109
  309.4 700.5 %all-reduce.3.cloned.1.call-done = f32[128,128]{1,0:T(8,128)} async-done(((f32[128,128]{1,0:T(8,128)}), f32[128,128]{1,0:T(8,128)}) %all-reduce.3.cloned.1.call-update) | async-done | bytes 65552 | tf_op jit(solution)/shard_map/psum | solution.py:109
  1009.9 1.5 copy.62
  (69 shorter events, 4.2 us)
Async XLA Ops:
  7.2 65.0 %copy-start = (bf16[14,4096]{1,0:T(8,128)(2,1)S(1)}, bf16[14,4096]{1,0:T(8,128)(2,1)}, u32[]{:S(2)}) copy-start(bf16[14,4096]{1,0:T(8,128)(2,1)} %param.12) | copy-start | bytes 344068
  7.2 1002.7 %all-reduce.3.cloned.1.call-start = ((), (), s32[]{:S(2)}) async-start(), calls=%async_computation | async-start | bytes 131072 | tf_op jit(solution)/shard_map/psum | solution.py:109
  8.0 25.7 %copy-start.13 = (s32[384]{0:T(512)}, s32[384]{0:T(512)S(1)}, u32[]{:S(2)}) copy-start(s32[384]{0:T(512)S(1)} %get-tuple-element.26) | copy-start | bytes 4612
  8.0 25.7 %copy-start.14 = (s32[384]{0:T(512)}, s32[384]{0:T(512)S(1)}, u32[]{:S(2)}) copy-start(s32[384]{0:T(512)S(1)} %get-tuple-element.27) | copy-start | bytes 4612
  8.0 48.1 %copy-start.11 = (s32[384]{0:T(512)}, s32[384]{0:T(512)S(1)}, u32[]{:S(2)}) copy-start(s32[384]{0:T(512)S(1)} %get-tuple-element.24) | copy-start | bytes 4612
  8.1 48.1 %copy-start.12 = (s32[384]{0:T(512)}, s32[384]{0:T(512)S(1)}, u32[]{:S(2)}) copy-start(s32[384]{0:T(512)S(1)} %get-tuple-element.25) | copy-start | bytes 4612
  8.1 55.2 %copy-start.9 = (s32[384]{0:T(512)}, s32[384]{0:T(512)S(1)}, u32[]{:S(2)}) copy-start(s32[384]{0:T(512)S(1)} %get-tuple-element.22) | copy-start | bytes 4612
  8.1 55.2 %copy-start.10 = (s32[384]{0:T(512)}, s32[384]{0:T(512)S(1)}, u32[]{:S(2)}) copy-start(s32[384]{0:T(512)S(1)} %get-tuple-element.23) | copy-start | bytes 4612
  8.1 60.3 %copy-start.8 = (s32[384]{0:T(512)}, s32[384]{0:T(512)S(1)}, u32[]{:S(2)}) copy-start(s32[384]{0:T(512)S(1)} %get-tuple-element.21) | copy-start | bytes 4612
  35.7 36.5 %copy-start.7 = (bf16[14,128]{1,0:T(8,128)(2,1)S(1)}, bf16[14,128]{1,0:T(8,128)(2,1)}, u32[]{:S(2)}) copy-start(bf16[14,128]{1,0:T(8,128)(2,1)} %param.16) | copy-start | bytes 10756
  35.7 40.6 %collective-permute-start = (f32[14,384]{0,1:T(8,128)}, f32[14,384]{0,1:T(8,128)}, u32[]{:S(2)}, u32[]{:S(2)}) collective-permute-start(f32[14,384]{0,1:T(8,128)} %multiply_bitcast_fusion.7), channel_id=1, source_target_pairs={{0,4},{4,8},{8,12},{12,16},{16,20},{20,24},{24,28},{28,32},{32,36}... | collective-permute-start | bytes 64520 | tf_op jit(solution)/shard_map/ppermute | solution.py:17
  42.2 35.4 %collective-permute-start.1 = (f32[14,384]{0,1:T(8,128)}, f32[14,384]{0,1:T(8,128)}, u32[]{:S(2)}, u32[]{:S(2)}) collective-permute-start(f32[14,384]{0,1:T(8,128)} %multiply_bitcast_fusion.6), channel_id=1, source_target_pairs={{4,0},{8,4},{12,8},{16,12},{20,16},{24,20},{28,24},{32,28},{36,32}... | collective-permute-start | bytes 64520 | tf_op jit(solution)/shard_map/ppermute | solution.py:17
  57.3 16.1 %copy-start.5 = (bf16[128,128]{1,0:T(8,128)(2,1)S(1)}, bf16[128,128]{1,0:T(8,128)(2,1)}, u32[]{:S(2)}) copy-start(bf16[128,128]{1,0:T(8,128)(2,1)} %param.18) | copy-start | bytes 98308
  58.1 25.2 %collective-permute-start.2 = (f32[14,384]{0,1:T(8,128)}, f32[14,384]{0,1:T(8,128)}, u32[]{:S(2)}, u32[]{:S(2)}) collective-permute-start(f32[14,384]{0,1:T(8,128)} %multiply_bitcast_fusion.5), channel_id=1, source_target_pairs={{0,16},{4,20},{8,24},{12,28},{16,32},{20,36},{24,40},{28,44},{32,4... | collective-permute-start | bytes 64520 | tf_op jit(solution)/shard_map/ppermute | solution.py:17
  62.0 35.8 %collective-permute-start.3 = (f32[14,384]{0,1:T(8,128)}, f32[14,384]{0,1:T(8,128)}, u32[]{:S(2)}, u32[]{:S(2)}) collective-permute-start(f32[14,384]{0,1:T(8,128)} %multiply_bitcast_fusion.4), channel_id=1, source_target_pairs={{16,0},{20,4},{24,8},{28,12},{32,16},{36,20},{40,24},{44,28},{48,3... | collective-permute-start | bytes 64520 | tf_op jit(solution)/shard_map/ppermute | solution.py:17
  65.2 36.9 %collective-permute-start.4 = (f32[14,384]{0,1:T(8,128)}, f32[14,384]{0,1:T(8,128)}, u32[]{:S(2)}, u32[]{:S(2)}) collective-permute-start(f32[14,384]{0,1:T(8,128)} %multiply_bitcast_fusion.3), channel_id=1, source_target_pairs={{0,20},{4,24},{8,28},{12,32},{16,36},{20,40},{24,44},{28,48},{32,5... | collective-permute-start | bytes 64520 | tf_op jit(solution)/shard_map/ppermute | solution.py:17
  71.4 13.2 %copy-start.19 = (f32[3,8]{1,0:T(4,128)S(1)}, f32[3,8]{1,0:T(4,128)}, u32[]{:S(2)}) copy-start(f32[3,8]{1,0:T(4,128)} %param.14) | copy-start | bytes 292
  76.3 30.3 %collective-permute-start.5 = (f32[14,384]{0,1:T(8,128)}, f32[14,384]{0,1:T(8,128)}, u32[]{:S(2)}, u32[]{:S(2)}) collective-permute-start(f32[14,384]{0,1:T(8,128)} %multiply_bitcast_fusion.2), channel_id=1, source_target_pairs={{20,0},{24,4},{28,8},{32,12},{36,16},{40,20},{44,24},{48,28},{52,3... | collective-permute-start | bytes 64520 | tf_op jit(solution)/shard_map/ppermute | solution.py:17
  77.6 33.5 %collective-permute-start.6 = (f32[14,384]{0,1:T(8,128)}, f32[14,384]{0,1:T(8,128)}, u32[]{:S(2)}, u32[]{:S(2)}) collective-permute-start(f32[14,384]{0,1:T(8,128)} %multiply_bitcast_fusion.1), channel_id=1, source_target_pairs={{0,12},{4,16},{8,20},{12,24},{16,28},{20,32},{24,36},{28,40},{32,4... | collective-permute-start | bytes 64520 | tf_op jit(solution)/shard_map/ppermute | solution.py:17
  83.3 32.3 %collective-permute-start.7 = (f32[14,384]{0,1:T(8,128)}, f32[14,384]{0,1:T(8,128)S(1)}, u32[]{:S(2)}, u32[]{:S(2)}) collective-permute-start(f32[14,384]{0,1:T(8,128)} %multiply_bitcast_fusion), channel_id=1, source_target_pairs={{12,0},{16,4},{20,8},{24,12},{28,16},{32,20},{36,24},{40,28},{44,3... | collective-permute-start | bytes 64520 | tf_op jit(solution)/shard_map/ppermute | solution.py:17
  120.5 1.7 copy-start.1
  120.5 1.8 copy-start.15
  122.3 0.8 copy-start.6
  125.6 4.9 copy-start.4
  130.5 3.6 copy-start.3
  134.0 3.6 copy-start.16
  134.0 3.6 copy-start.17
  134.0 3.6 copy-start.18
  134.0 4.2 copy-start.2
Sparse Core Ops, SparseCore 0:
  138.6 871.2 all-reduce.2
where the time goes:
time: 1020 us
  waiting for transfers between devices  701 us (69%)
  blocking collectives  170 us (17%)
  other arithmetic  65.1 us (6%)
  starting transfers between devices  32 us (3%)
  matrix products  20.7 us (2%)
  local copies, waits for them, and re-layouts  15.8 us (2%)
  between operations  14.6 us (1%)
    psum x1, waiting for transfers between devices, per_device(): summed = lax.psum((grad_in, grad_mid, grad_out), ('graph', 'group'))  700 us
    psum x1, blocking collectives, per_device(): summed = lax.psum((grad_in, grad_mid, grad_out), ('graph', 'group'))  170 us
    scatter-add x8, other arithmetic, per_device(): assembled.at[:, safe[deposit_which]]  34.6 us
    ppermute x8, starting transfers between devices, from_behind(): return lax.ppermute(block, axis, route)  32 us
  transfers between devices with their start and end apart: 9, of which 1 were waited for; matrix products, arithmetic and copies ran while one was open for 5% of the time, Pallas kernels for 0%

commit v1 on v0

v1 whole, which is shorter than its diff:
```python
import jax
import jax.numpy as jnp
import numpy as np
import ml_dtypes
from jax import lax
from jax.experimental import pallas as pl
from jax.experimental.pallas import tpu as pltpu
from jax.sharding import PartitionSpec as P

FIELDS = 14
ROWS = 16
HIDDEN = 128
NODES = 512
ELEMS = 8
LANES = 128
LOCAL = ELEMS * NODES
CHUNKS = LOCAL // LANES
PROWS = 4
SLOTS = 384
FACE_BLOCKS = 12
BLOCKS = 14
PIECE = 5
MESH = pl.DeviceIdType.MESH
OFFSETS = (1, -1, PROWS, -PROWS, PROWS + 1, -PROWS - 1, PROWS - 1, -PROWS + 1)
ZBLOCK = 4

step_scale = 0.5


def stiffness_table():
    order = 7
    points = np.cos(np.pi * np.arange(order + 1) / order)
    ends = np.ones(order + 1)
    ends[0] = 2.0
    ends[-1] = 2.0
    deriv = np.zeros((order + 1, order + 1))
    for first in range(order + 1):
        for second in range(order + 1):
            if first != second:
                deriv[first, second] = (
                    ends[first]
                    / ends[second]
                    * (-1.0) ** (first + second)
                    / (points[first] - points[second])
                )
    row_sums = deriv.sum(axis=1)
    for place in range(order + 1):
        deriv[place, place] = -row_sums[place]
    return deriv.T @ deriv


def split_table(table):
    high = table.astype(ml_dtypes.bfloat16)
    low = (table - high.astype(np.float64)).astype(ml_dtypes.bfloat16)
    return np.stack([high, low])


def direction_tables():
    table = stiffness_table()
    along_one = np.kron(table, np.eye(64)).T
    along_two = np.kron(np.eye(2), np.kron(table, np.eye(8))).T
    along_three = np.kron(np.eye(16), table).T
    return split_table(along_one), split_table(np.concatenate([along_two, along_three], axis=1))


def pick(block, places):
    return jnp.take_along_axis(block, places, axis=1, mode="promise_in_bounds")


def contract(left, right, left_dim, right_dim):
    return lax.dot_general(
        left,
        right,
        (((left_dim,), (right_dim,)), ((), ())),
        preferred_element_type=jnp.float32,
    )


def span(which, size):
    return pl.ds(pl.multiple_of(which * size, size), size)


def body(
    state,
    cot,
    diff,
    lists,
    w_in,
    b_in,
    w_mid,
    b_mid,
    w_out,
    one_hbm,
    two_three,
    out,
    gin,
    gmid,
    gout,
    cot16,
    send_idx,
    send_blocks,
    face_in,
    diag_in,
    slot_high,
    slot_low,
    inv_block,
    inv_lane,
    asm,
    firsts,
    seconds,
    back_firsts,
    grads,
    pieces,
    rs1,
    rs2,
    mine,
    ring_a,
    ring_b,
    final,
    one_vmem,
    table_sem,
    halo_send,
    halo_recv,
    rs1_send,
    rs1_recv,
    rs2_send,
    rs2_recv,
    a_send,
    a_recv,
    b_send,
    b_recv,
    g1_send,
    g1_recv,
    g2_send,
    g2_recv,
    far_one,
    far_two,
):
    graph = lax.axis_index("graph")
    x = lax.axis_index("group")
    z = graph // 8
    q = graph % 8
    zl = z % ZBLOCK
    zh = z // ZBLOCK
    outer = 32 // ZBLOCK

    def place(z_at, q_at, x_at):
        return {"graph": z_at * 8 + q_at, "group": x_at}

    def beside(offset):
        return {"graph": (graph + offset + 256) % 256, "group": x}

    def in_plane(d):
        return place(z, (q + d) % 8, x)

    def along_x(d):
        return place(z, q, (x + d) % 4)

    def in_block(d):
        return place(zh * ZBLOCK + (zl + d) % ZBLOCK, q, x)

    def across(d):
        return place(((zh + d) % outer) * ZBLOCK + zl, q, x)

    def along_z(d):
        return place((z + d + 32) % 32, q, x)

    table_copy = pltpu.make_async_copy(one_hbm, one_vmem, table_sem)
    table_copy.start()

    barrier = pltpu.get_barrier_semaphore()
    near = [beside(o) for o in OFFSETS]
    near += [in_plane(d) for d in range(1, 8)]
    near += [along_x(d) for d in range(1, 4)]
    near += [in_block(d) for d in range(1, ZBLOCK)]
    near += [along_z(4), along_z(-4)]
    for target in near:
        pl.semaphore_signal(barrier, inc=1, device_id=target, device_id_type=MESH)

    cot16[0:FIELDS, :] = cot[0]
    cot16[FIELDS:ROWS, :] = jnp.zeros((ROWS - FIELDS, LOCAL), jnp.float32)
    lane = lax.broadcasted_iota(jnp.int32, (1, LANES), 1)
    leading = lane < 64

    def list_row(which, block):
        return lists[0, which : which + 1, block * LANES : (block + 1) * LANES]

    sent, received = [], []
    for b in range(FACE_BLOCKS):
        row = list_row(b // 3, b % 3)
        sent.append(row)
        received.append(row)
    for k in (4, 6):
        low, high = list_row(k, 0), list_row(k + 1, 0)
        sent.append(jnp.where(leading, low, pltpu.roll(high, 64, 1)))
        received.append(jnp.where(leading, high, pltpu.roll(low, 64, 1)))
    for b in range(BLOCKS):
        send_idx[b] = jnp.broadcast_to(sent[b], (8, LANES))

    def gather_block(b, carry):
        idx = send_idx[b]
        low = jnp.bitwise_and(idx, LANES - 1)
        high = jnp.right_shift(idx, 7)
        top = jnp.zeros((8, LANES), jnp.float32)
        bottom = jnp.zeros((8, LANES), jnp.float32)
        for h in range(CHUNKS):
            match = high == h
            lanes = slice(h * LANES, (h + 1) * LANES)
            top = jnp.where(match, pick(cot16[0:8, lanes], low), top)
            bottom = jnp.where(match, pick(cot16[8:16, lanes], low), bottom)
        send_blocks[b, 0:8] = top
        send_blocks[b, 8:16] = bottom
        return carry

    lax.fori_loop(0, BLOCKS, gather_block, 0)

    pl.semaphore_wait(barrier, len(near))
    halo = []
    for k in range(8):
        if k < 4:
            source = send_blocks.at[3 * k : 3 * k + 3]
            target = face_in.at[3 * (k ^ 1) : 3 * (k ^ 1) + 3]
        else:
            source = send_blocks.at[FACE_BLOCKS + (k - 4) // 2]
            target = diag_in.at[(k ^ 1) - 4]
        copy = pltpu.make_async_remote_copy(
            src_ref=source,
            dst_ref=target,
            send_sem=halo_send.at[k],
            recv_sem=halo_recv.at[k ^ 1],
            device_id=beside(OFFSETS[k]),
            device_id_type=MESH,
        )
        copy.start()
        halo.append(copy)
    for d in (4, -4):
        pl.semaphore_signal(far_one, inc=1, device_id=along_z(d), device_id_type=MESH)

    lane_f = lane.astype(jnp.float32)
    rows32 = lax.broadcasted_iota(jnp.int32, (CHUNKS, LANES), 0)
    rows128 = lax.broadcasted_iota(jnp.int32, (LANES, LANES), 0)
    for b in range(BLOCKS):
        low = jnp.bitwise_and(received[b], LANES - 1)
        high = jnp.right_shift(received[b], 7)
        match = rows32 == high
        lanes = slice(b * LANES, (b + 1) * LANES)
        slot_high[0:32, lanes] = jnp.where(match, float(b + 1), 0.0).astype(jnp.bfloat16)
        slot_high[32:64, lanes] = jnp.where(match, lane_f, 0.0).astype(jnp.bfloat16)
        slot_low[:, lanes] = jnp.where(rows128 == low, 1.0, 0.0).astype(jnp.bfloat16)
    inverse = contract(slot_high[...], slot_low[...], 1, 1).astype(jnp.int32)
    for h in range(CHUNKS):
        inv_block[h] = jnp.broadcast_to(inverse[h : h + 1], (8, LANES))
        inv_lane[h] = jnp.broadcast_to(inverse[32 + h : 33 + h], (8, LANES))

    bias_in = jnp.broadcast_to(b_in[...].reshape(1, HIDDEN), (HIDDEN, HIDDEN)).T[:, 0:1]
    bias_mid = jnp.broadcast_to(b_mid[...].reshape(1, HIDDEN), (HIDDEN, HIDDEN)).T[:, 0:1]

    def forward(e, carry):
        inputs = state[:, span(e, NODES)]
        first = jnp.tanh(contract(w_in[...], inputs, 0, 0) + bias_in).astype(jnp.bfloat16)
        firsts[e] = first
        second = jnp.tanh(contract(w_mid[...], first, 0, 0) + bias_mid).astype(jnp.bfloat16)
        seconds[e] = second
        return carry

    lax.fori_loop(0, ELEMS, forward, 0)

    pl.semaphore_wait(far_one, 2)
    for d in (8, -8):
        pl.semaphore_signal(far_two, inc=1, device_id=along_z(d), device_id_type=MESH)

    for copy in halo:
        copy.wait_recv()

    def assemble(h, carry):
        where_block = inv_block[h]
        where_lane = inv_lane[h]
        top = jnp.zeros((8, LANES), jnp.float32)
        bottom = jnp.zeros((8, LANES), jnp.float32)
        for b in range(BLOCKS):
            match = where_block == b + 1
            if b < FACE_BLOCKS:
                upper, lower = face_in[b, 0:8], face_in[b, 8:16]
            else:
                k = 2 * (b - FACE_BLOCKS)
                upper = jnp.where(leading, diag_in[k + 1, 0:8], diag_in[k, 0:8])
                lower = jnp.where(leading, diag_in[k + 1, 8:16], diag_in[k, 8:16])
            top = jnp.where(match, pick(upper, where_lane), top)
            bottom = jnp.where(match, pick(lower, where_lane), bottom)
        shared = where_block > 0
        own = cot16[0:8, span(h, LANES)]
        asm[0:8, span(h, LANES)] = jnp.where(shared, 0.5 * own + 0.5 * top, own)
        own = cot16[8:16, span(h, LANES)]
        asm[8:16, span(h, LANES)] = jnp.where(shared, 0.5 * own + 0.5 * bottom, own)
        return carry

    lax.fori_loop(0, CHUNKS, assemble, 0)

    grads[...] = jnp.zeros_like(grads)

    def backward(e, carry):
        here = span(e, NODES)
        impulse = (step_scale * asm[0:FIELDS, here]).astype(jnp.bfloat16)
        first, second = firsts[e], seconds[e]
        wide = second.astype(jnp.float32)
        back_second = contract(w_out[...], impulse, 1, 0) * (1.0 - wide * wide)
        back_second = back_second.astype(jnp.bfloat16)
        wide = first.astype(jnp.float32)
        back_first = contract(w_mid[...], back_second, 1, 0) * (1.0 - wide * wide)
        back_first = back_first.astype(jnp.bfloat16)
        back_firsts[e] = back_first
        grads[0:128] += contract(first, back_second, 1, 1)
        grads[128 : 128 + FIELDS] += contract(state[:, here], back_first, 1, 1)
        grads[144 : 144 + FIELDS] += contract(impulse, second, 1, 1)
        return carry

    lax.fori_loop(0, ELEMS, backward, 0)

    for r in range(32):
        pieces[r // 4, r % 4] = grads[PIECE * r : PIECE * (r + 1)]
    sends = []

    def push(source, target, send_sem, recv_sem, device):
        copy = pltpu.make_async_remote_copy(
            src_ref=source,
            dst_ref=target,
            send_sem=send_sem,
            recv_sem=recv_sem,
            device_id=device,
            device_id_type=MESH,
        )
        copy.start()
        sends.append(copy)
        return copy

    arriving = [
        push(pieces.at[(q + d) % 8], rs1.at[d - 1], rs1_send.at[d - 1], rs1_recv.at[d - 1], in_plane(d))
        for d in range(1, 8)
    ]
    total = pieces[q]
    for d in range(1, 8):
        arriving[d - 1].wait_recv()
        total = total + rs1[d - 1]
    mine[...] = total
    arriving = [
        push(mine.at[(x + d) % 4], rs2.at[d - 1], rs2_send.at[d - 1], rs2_recv.at[d - 1], along_x(d))
        for d in range(1, 4)
    ]
    total = mine[x]
    for d in range(1, 4):
        arriving[d - 1].wait_recv()
        total = total + rs2[d - 1]

    ring_a[zl] = total
    arriving = [
        push(ring_a.at[zl], ring_a.at[zl], a_send.at[d - 1], a_recv.at[d - 1], in_block(d))
        for d in range(1, ZBLOCK)
    ]
    for copy in arriving:
        copy.wait_recv()
    total = ring_a[0]
    for d in range(1, ZBLOCK):
        total = total + ring_a[d]
    ring_b[zh] = total
    pl.semaphore_wait(far_two, 2)
    across_z = [
        push(ring_b.at[zh], ring_b.at[zh], b_send.at[d - 1], b_recv.at[d - 1], across(d))
        for d in range(1, outer)
    ]

    table_copy.wait()
    rows = jnp.concatenate([asm[:, e * NODES : (e + 1) * NODES] for e in range(ELEMS)], axis=0)
    high = rows.astype(jnp.bfloat16)
    low = (rows - high.astype(jnp.float32)).astype(jnp.bfloat16)
    along_one = (
        contract(high, one_vmem[0], 1, 0)
        + contract(low, one_vmem[0], 1, 0)
        + contract(high, one_vmem[1], 1, 0)
    )
    for e in range(ELEMS):
        toward = contract(w_in[...], back_firsts[e], 1, 0)
        for part in range(NODES // LANES):
            lanes = slice(part * LANES, (part + 1) * LANES)
            high_here = high[e * ROWS : (e + 1) * ROWS, lanes]
            low_here = low[e * ROWS : (e + 1) * ROWS, lanes]
            others = (
                contract(high_here, two_three[0], 1, 0)
                + contract(low_here, two_three[0], 1, 0)
                + contract(high_here, two_three[1], 1, 0)
            )
            viscous = -(
                diff[0, e] * along_one[e * ROWS : (e + 1) * ROWS, lanes]
                + diff[1, e] * others[:, 0:LANES]
                + diff[2, e] * others[:, LANES:]
            )
            here = slice(e * NODES + part * LANES, e * NODES + (part + 1) * LANES)
            value = asm[:, here] + step_scale * viscous
            out[0, :, here] = value[0:FIELDS] + toward[:, lanes]

    for copy in across_z:
        copy.wait_recv()
    total = ring_b[0]
    for d in range(1, outer):
        total = total + ring_b[d]

    final[q, x] = total
    arriving = [
        push(final.at[q, x], final.at[q, x], g1_send.at[d - 1], g1_recv.at[d - 1], along_x(d))
        for d in range(1, 4)
    ]
    for copy in arriving:
        copy.wait_recv()
    arriving = [
        push(final.at[q], final.at[q], g2_send.at[d - 1], g2_recv.at[d - 1], in_plane(d))
        for d in range(1, 8)
    ]
    for copy in arriving:
        copy.wait_recv()
    for r in range(32):
        grads[PIECE * r : PIECE * (r + 1)] = final[r // 4, r % 4]
    gmid[...] = grads[0:128]
    gin[...] = grads[128 : 128 + FIELDS]
    gout[...] = grads[144:160].T[:, 0:FIELDS]

    for copy in halo + sends:
        copy.wait_send()


def per_device(state, cotangent, diffusivity, shared_nodes, w_in, b_in, w_mid, b_mid, w_out):
    f32, bf16 = jnp.float32, jnp.bfloat16
    one, two_three = direction_tables()
    vmem = pl.BlockSpec(memory_space=pltpu.VMEM)
    dma = pltpu.SemaphoreType.DMA
    outer = 32 // ZBLOCK
    return pl.pallas_call(
        body,
        out_shape=(
            jax.ShapeDtypeStruct((1, FIELDS, LOCAL), f32),
            jax.ShapeDtypeStruct((FIELDS, HIDDEN), f32),
            jax.ShapeDtypeStruct((HIDDEN, HIDDEN), f32),
            jax.ShapeDtypeStruct((HIDDEN, FIELDS), f32),
        ),
        in_specs=[vmem, vmem, pl.BlockSpec(memory_space=pltpu.SMEM)]
        + [vmem] * 6
        + [pl.BlockSpec(memory_space=pl.ANY), vmem],
        out_specs=(vmem, vmem, vmem, vmem),
        scratch_shapes=[
            pltpu.VMEM((ROWS, LOCAL), f32),
            pltpu.VMEM((BLOCKS, 8, LANES), jnp.int32),
            pltpu.VMEM((BLOCKS, ROWS, LANES), f32),
            pltpu.VMEM((FACE_BLOCKS, ROWS, LANES), f32),
            pltpu.VMEM((4, ROWS, LANES), f32),
            pltpu.VMEM((64, BLOCKS * LANES), bf16),
            pltpu.VMEM((LANES, BLOCKS * LANES), bf16),
            pltpu.VMEM((CHUNKS, 8, LANES), jnp.int32),
            pltpu.VMEM((CHUNKS, 8, LANES), jnp.int32),
            pltpu.VMEM((ROWS, LOCAL), f32),
            pltpu.VMEM((ELEMS, HIDDEN, NODES), bf16),
            pltpu.VMEM((ELEMS, HIDDEN, NODES), bf16),
            pltpu.VMEM((ELEMS, HIDDEN, NODES), bf16),
            pltpu.VMEM((160, HIDDEN), f32),
            pltpu.VMEM((8, 4, PIECE, LANES), f32),
            pltpu.VMEM((7, 4, PIECE, LANES), f32),
            pltpu.VMEM((3, PIECE, LANES), f32),
            pltpu.VMEM((4, PIECE, LANES), f32),
            pltpu.VMEM((ZBLOCK, PIECE, LANES), f32),
            pltpu.VMEM((outer, PIECE, LANES), f32),
            pltpu.VMEM((8, 4, PIECE, LANES), f32),
            pltpu.VMEM((2, NODES, NODES), bf16),
            dma,
            dma((8,)),
            dma((8,)),
            dma((7,)),
            dma((7,)),
            dma((3,)),
            dma((3,)),
            dma((ZBLOCK - 1,)),
            dma((ZBLOCK - 1,)),
            dma((outer - 1,)),
            dma((outer - 1,)),
            dma((3,)),
            dma((3,)),
            dma((7,)),
            dma((7,)),
            pltpu.SemaphoreType.REGULAR,
            pltpu.SemaphoreType.REGULAR,
        ],
        compiler_params=pltpu.CompilerParams(
            collective_id=0, has_side_effects=True, vmem_limit_bytes=32 * 1024 * 1024
        ),
    )(
        state,
        cotangent,
        diffusivity,
        shared_nodes,
        w_in,
        b_in,
        w_mid,
        b_mid,
        w_out,
        jnp.asarray(one),
        jnp.asarray(two_three),
    )


def solution(mesh):
    in_specs = (
        P(None, "graph"),
        P("group", None, "graph"),
        P(None, "graph"),
        P("graph", None, None),
        P(),
        P(),
        P(),
        P(),
        P(),
    )
    out_specs = (P("group", None, "graph"), P(), P(), P())
    return jax.shard_map(
        per_device, mesh=mesh, in_specs=in_specs, out_specs=out_specs, check_vma=False
    )
```

time: 1020 us -> 73.3 us (0.07)
  waiting for transfers between devices: 701 us -> 0 us
  blocking collectives: 170 us -> 0 us
  Pallas kernels: 0 us -> 66.2 us
  other arithmetic: 65.1 us -> 0 us
  starting transfers between devices: 32 us -> 0 us
  matrix products: 20.7 us -> 0 us
  between operations: 14.6 us -> 0.77 us
    psum x1 -> x0, waiting for transfers between devices: 700 us -> none  [per_device(): summed = lax.psum((grad_in, grad_mid, grad_out), ('graph', 'group'))]
    psum x1 -> x0, blocking collectives: 170 us -> none  [per_device(): summed = lax.psum((grad_in, grad_mid, grad_out), ('graph', 'group'))]
    pallas_call x0 -> x1, Pallas kernels: none -> 66.2 us  [per_device(): pl.pallas_call(body, out_shape=(jax.ShapeDtypeStruct((1, FIELDS, LOCAL),...]
    scatter-add x8 -> x0, other arithmetic: 34.6 us -> none  [per_device(): assembled.at[:, safe[deposit_which]]]
    ppermute x8 -> x0, starting transfers between devices: 32 us -> none  [from_behind(): return lax.ppermute(block, axis, route)]
    dot_general x11 -> x0, matrix products: 20.7 us -> none  [the longest x3 12 us: diffuse(): jnp.dot(rows, matrix, precision=highest).reshape(fields, elements, NODES)]
    another operation x1 -> x0, other arithmetic: 20.2 us -> none  [per_device(): jnp.zeros((local,), jnp.float32).at[safe.reshape(-1)].max(valid.reshape(-1))]
  transfers between devices with their start and end apart: 9 -> 0, of which waited for: 1 -> 0; matrix products, arithmetic and copies ran while one was open for 5% -> 0% of each run, Pallas kernels for 0% -> 0%
where the time goes in v1:
time: 73.3 us; the launch traced here: 73.1 us
  Pallas kernels  66.2 us (90%)
  local copies, waits for them, and re-layouts  6.12 us (8%)
  between operations  0.77 us (1%)
    pallas_call x1, Pallas kernels, per_device(): pl.pallas_call(body, out_shape=(jax.ShapeDtypeStruct((1, FIELDS, LOCAL),...  66.2 us
    unnamed x22, local copies, waits for them, and re-layouts  4.52 us
    pallas_call x2, local copies, waits for them, and re-layouts, per_device(): pl.pallas_call(body, out_shape=(jax.ShapeDtypeStruct((1, FIELDS, LOCAL),...  1.6 us

profile of v1, /device:TPU:1, one launch (start us, length us, event | category | flops | bytes accessed | tf_op | source)
XLA Modules:
  0.0 73.1 jit_solution(12896325135744070346)
XLA Ops:
  0.6 0.8 %copy.16.w_out = bf16[128,14]{1,0:T(8,128)(2,1)S(1)} copy(bf16[128,14]{0,1:T(8,128)(2,1)} %param.19) | data formatting | bytes 7168 | tf_op args[8]
  1.4 0.0 copy-start.1
  1.4 0.0 copy-start.2
  1.5 0.0 copy-start.3
  1.5 0.0 copy-start.4
  1.5 0.0 copy-start.5
  1.5 0.0 copy-start.6
  1.5 0.0 copy-start.7
  1.5 0.0 copy-start.8
  1.5 1.2 %copy.15.cot = f32[1,14,4096]{2,1,0:T(8,128)S(1)} copy(f32[1,14,4096]{2,0,1:T(1,128)} %param.12) | data formatting | bytes 458752 | tf_op args[1]
  2.7 0.0 copy-done.1
  2.8 0.0 copy-done.2
  2.8 0.0 copy-done.3
  2.8 0.0 copy-done.4
  2.8 0.0 copy-done.5
  2.8 0.0 copy-done.6
  2.8 0.0 copy-done.7
  2.8 0.0 copy-done.8
  2.8 0.0 copy-start
  2.8 1.2 %copy-done = bf16[2,512,512]{2,1,0:T(8,128)(2,1)S(1)} copy-done((bf16[2,512,512]{2,1,0:T(8,128)(2,1)S(1)}, bf16[2,512,512]{2,1,0:T(8,128)(2,1)}, u32[]{:S(2)}) %copy-start) | copy-done | bytes 1048600
  4.1 66.2 %shard_map.138 = (f32[1,14,4096]{2,1,0:T(8,128)S(1)}, f32[14,128]{1,0:T(8,128)S(1)}, f32[128,128]{1,0:T(8,128)S(1)}, f32[128,14]{1,0:T(8,128)S(1)}) custom-call(bf16[14,4096]{1,0:T(8,128)(2,1)S(1)} %copy-done.1, f32[1,14,4096]{2,1,0:T(8,128)S(1)} %copy.15.cot, f32[3,8]{1,0:T(4,128)S(1)} %copy-done.6, s32[1,8,384]{2,1,0:T(8,128)S(1)} %copy-done.4, ...), custom_call_target="tpu_custom_call" | custom-call | tf_op jit(solution)/shard_map/pallas_call | solution.py:435
  70.3 0.9 %copy.17 = f32[1,14,4096]{2,0,1:T(1,128)} copy(f32[1,14,4096]{2,1,0:T(8,128)S(1)} %get-tuple-element.4) | data formatting | bytes 458752 | tf_op jit(solution)/shard_map/pallas_call | solution.py:435
  71.2 0.7 copy.18
  71.9 0.6 copy.21
  72.5 0.6 copy.22
Async XLA Ops:
  1.4 1.3 %copy-start.1 = (bf16[14,4096]{1,0:T(8,128)(2,1)S(1)}, bf16[14,4096]{1,0:T(8,128)(2,1)}, u32[]{:S(2)}) copy-start(bf16[14,4096]{1,0:T(8,128)(2,1)} %state.1) | copy-start | bytes 344068
  1.4 1.3 %copy-start.2 = (bf16[2,128,256]{2,1,0:T(8,128)(2,1)S(1)}, bf16[2,128,256]{2,1,0:T(8,128)(2,1)}, u32[]{:S(2)}) copy-start(bf16[2,128,256]{2,1,0:T(8,128)(2,1)} %constant.5.clone.two_three) | copy-start | bytes 393220
  1.5 1.3 %copy-start.3 = (bf16[128,128]{1,0:T(8,128)(2,1)S(1)}, bf16[128,128]{1,0:T(8,128)(2,1)}, u32[]{:S(2)}) copy-start(bf16[128,128]{1,0:T(8,128)(2,1)} %w_mid.1) | copy-start | bytes 98308
  1.5 1.3 %copy-start.4 = (s32[1,8,384]{2,1,0:T(8,128)S(1)}, s32[1,8,384]{2,1,0:T(8,128)}, u32[]{:S(2)}) copy-start(s32[1,8,384]{2,1,0:T(8,128)} %lists.1) | copy-start | bytes 36868
  1.5 1.3 %copy-start.5 = (bf16[14,128]{1,0:T(8,128)(2,1)S(1)}, bf16[14,128]{1,0:T(8,128)(2,1)}, u32[]{:S(2)}) copy-start(bf16[14,128]{1,0:T(8,128)(2,1)} %w_in.1) | copy-start | bytes 10756
  1.5 1.3 %copy-start.6 = (f32[3,8]{1,0:T(4,128)S(1)}, f32[3,8]{1,0:T(4,128)}, u32[]{:S(2)}) copy-start(f32[3,8]{1,0:T(4,128)} %diff.1) | copy-start | bytes 292
  1.5 1.3 %copy-start.7 = (f32[128]{0:T(128)S(1)}, f32[128]{0:T(128)}, u32[]{:S(2)}) copy-start(f32[128]{0:T(128)} %b_in.1) | copy-start | bytes 1540
  1.5 1.3 %copy-start.8 = (f32[128]{0:T(128)S(1)}, f32[128]{0:T(128)}, u32[]{:S(2)}) copy-start(f32[128]{0:T(128)} %b_mid.1) | copy-start | bytes 1540
  2.8 1.2 %copy-start = (bf16[2,512,512]{2,1,0:T(8,128)(2,1)S(1)}, bf16[2,512,512]{2,1,0:T(8,128)(2,1)}, u32[]{:S(2)}) copy-start(bf16[2,512,512]{2,1,0:T(8,128)(2,1)} %constant.4.clone.one_hbm) | copy-start | bytes 3145732

commit v2 on v1

--- a/solution.py
+++ b/solution.py
@@ -22,7 +22,9 @@
 PIECE = 5
 MESH = pl.DeviceIdType.MESH
 OFFSETS = (1, -1, PROWS, -PROWS, PROWS + 1, -PROWS - 1, PROWS - 1, -PROWS + 1)
-ZBLOCK = 4
+ZBLOCK = 1
+OUTER = 32 // ZBLOCK
+NEAR_Z = (1, 2, 3, 4, -1, -2, -3, -4)
 
 step_scale = 0.5
 
@@ -81,6 +83,19 @@
 
 
 def body(
+    state_hbm,
+    cot_hbm,
+    diff_hbm,
+    lists_hbm,
+    w_in_hbm,
+    b_in_hbm,
+    w_mid_hbm,
+    b_mid_hbm,
+    w_out_hbm,
+    one_hbm,
+    two_three_hbm,
+    out,
+    final,
     state,
     cot,
     diff,
@@ -90,12 +105,8 @@
     w_mid,
     b_mid,
     w_out,
-    one_hbm,
+    one,
     two_three,
-    out,
-    gin,
-    gmid,
-    gout,
     cot16,
     send_idx,
     send_blocks,
@@ -111,28 +122,20 @@
     back_firsts,
     grads,
     pieces,
-    rs1,
-    rs2,
-    mine,
+    plane_in,
     ring_a,
     ring_b,
-    final,
-    one_vmem,
-    table_sem,
+    fetched,
     halo_send,
     halo_recv,
-    rs1_send,
-    rs1_recv,
-    rs2_send,
-    rs2_recv,
+    rs_send,
+    rs_recv,
     a_send,
     a_recv,
     b_send,
     b_recv,
-    g1_send,
-    g1_recv,
-    g2_send,
-    g2_recv,
+    g_send,
+    g_recv,
     far_one,
     far_two,
 ):
@@ -140,9 +143,9 @@
     x = lax.axis_index("group")
     z = graph // 8
     q = graph % 8
+    rank = x * 8 + q
     zl = z % ZBLOCK
     zh = z // ZBLOCK
-    outer = 32 // ZBLOCK
 
     def place(z_at, q_at, x_at):
         return {"graph": z_at * 8 + q_at, "group": x_at}
@@ -151,34 +154,54 @@
         return {"graph": (graph + offset + 256) % 256, "group": x}
 
     def in_plane(d):
-        return place(z, (q + d) % 8, x)
-
-    def along_x(d):
-        return place(z, q, (x + d) % 4)
+        other = (rank + d) % 32
+        return place(z, other % 8, other // 8)
 
     def in_block(d):
         return place(zh * ZBLOCK + (zl + d) % ZBLOCK, q, x)
 
     def across(d):
-        return place(((zh + d) % outer) * ZBLOCK + zl, q, x)
+        return place(((zh + d) % OUTER) * ZBLOCK + zl, q, x)
 
     def along_z(d):
         return place((z + d + 32) % 32, q, x)
 
-    table_copy = pltpu.make_async_copy(one_hbm, one_vmem, table_sem)
-    table_copy.start()
+    def signal(semaphore, target):
+        pl.semaphore_signal(semaphore, inc=1, device_id=target, device_id_type=MESH)
+
+    fetches = [
+        pltpu.make_async_copy(source, target, fetched.at[i])
+        for i, (source, target) in enumerate(
+            (
+                (cot_hbm, cot),
+                (lists_hbm, lists),
+                (state_hbm, state),
+                (w_in_hbm, w_in),
+                (b_in_hbm, b_in),
+                (w_mid_hbm, w_mid),
+                (b_mid_hbm, b_mid),
+                (w_out_hbm, w_out),
+                (diff_hbm, diff),
+                (one_hbm, one),
+                (two_three_hbm, two_three),
+            )
+        )
+    ]
+    for fetch in fetches:
+        fetch.start()
 
     barrier = pltpu.get_barrier_semaphore()
     near = [beside(o) for o in OFFSETS]
-    near += [in_plane(d) for d in range(1, 8)]
-    near += [along_x(d) for d in range(1, 4)]
-    near += [in_block(d) for d in range(1, ZBLOCK)]
-    near += [along_z(4), along_z(-4)]
+    near += [along_z(d) for d in NEAR_Z]
+    near += [in_plane(d) for d in range(1, 32)]
     for target in near:
-        pl.semaphore_signal(barrier, inc=1, device_id=target, device_id_type=MESH)
-
-    cot16[0:FIELDS, :] = cot[0]
+        signal(barrier, target)
+
+    fetches[0].wait()
+    for h in range(CHUNKS):
+        cot16[0:FIELDS, h * LANES : (h + 1) * LANES] = cot[pl.ds(h, FIELDS, stride=CHUNKS), :]
     cot16[FIELDS:ROWS, :] = jnp.zeros((ROWS - FIELDS, LOCAL), jnp.float32)
+    fetches[1].wait()
     lane = lax.broadcasted_iota(jnp.int32, (1, LANES), 1)
     leading = lane < 64
 
@@ -212,29 +235,35 @@
         send_blocks[b, 8:16] = bottom
         return carry
 
-    lax.fori_loop(0, BLOCKS, gather_block, 0)
-
-    pl.semaphore_wait(barrier, len(near))
-    halo = []
-    for k in range(8):
-        if k < 4:
-            source = send_blocks.at[3 * k : 3 * k + 3]
-            target = face_in.at[3 * (k ^ 1) : 3 * (k ^ 1) + 3]
-        else:
-            source = send_blocks.at[FACE_BLOCKS + (k - 4) // 2]
-            target = diag_in.at[(k ^ 1) - 4]
+    lax.fori_loop(0, BLOCKS, gather_block, 0, unroll=2)
+
+    sends = []
+
+    def push(source, target, send_sem, recv_sem, device):
         copy = pltpu.make_async_remote_copy(
             src_ref=source,
             dst_ref=target,
-            send_sem=halo_send.at[k],
-            recv_sem=halo_recv.at[k ^ 1],
-            device_id=beside(OFFSETS[k]),
+            send_sem=send_sem,
+            recv_sem=recv_sem,
+            device_id=device,
             device_id_type=MESH,
         )
         copy.start()
-        halo.append(copy)
+        sends.append(copy)
+        return copy
+
+    pl.semaphore_wait(barrier, len(near))
+    halo = []
+    for k in (2, 3, 0, 1, 4, 5, 6, 7):
+        if k < 4:
+            source = send_blocks.at[3 * k : 3 * k + 3, 0:FIELDS]
+            target = face_in.at[3 * (k ^ 1) : 3 * (k ^ 1) + 3, 0:FIELDS]
+        else:
+            source = send_blocks.at[FACE_BLOCKS + (k - 4) // 2, 0:FIELDS]
+            target = diag_in.at[(k ^ 1) - 4, 0:FIELDS]
+        halo.append(push(source, target, halo_send.at[k], halo_recv.at[k ^ 1], beside(OFFSETS[k])))
     for d in (4, -4):
-        pl.semaphore_signal(far_one, inc=1, device_id=along_z(d), device_id_type=MESH)
+        signal(far_one, along_z(d))
 
     lane_f = lane.astype(jnp.float32)
     rows32 = lax.broadcasted_iota(jnp.int32, (CHUNKS, LANES), 0)
@@ -252,6 +281,8 @@
         inv_block[h] = jnp.broadcast_to(inverse[h : h + 1], (8, LANES))
         inv_lane[h] = jnp.broadcast_to(inverse[32 + h : 33 + h], (8, LANES))
 
+    for fetch in fetches[2:8]:
+        fetch.wait()
     bias_in = jnp.broadcast_to(b_in[...].reshape(1, HIDDEN), (HIDDEN, HIDDEN)).T[:, 0:1]
     bias_mid = jnp.broadcast_to(b_mid[...].reshape(1, HIDDEN), (HIDDEN, HIDDEN)).T[:, 0:1]
 
@@ -267,7 +298,7 @@
 
     pl.semaphore_wait(far_one, 2)
     for d in (8, -8):
-        pl.semaphore_signal(far_two, inc=1, device_id=along_z(d), device_id_type=MESH)
+        signal(far_two, along_z(d))
 
     for copy in halo:
         copy.wait_recv()
@@ -294,7 +325,7 @@
         asm[8:16, span(h, LANES)] = jnp.where(shared, 0.5 * own + 0.5 * bottom, own)
         return carry
 
-    lax.fori_loop(0, CHUNKS, assemble, 0)
+    lax.fori_loop(0, CHUNKS, assemble, 0, unroll=2)
 
     grads[...] = jnp.zeros_like(grads)
 
@@ -303,7 +334,7 @@
         impulse = (step_scale * asm[0:FIELDS, here]).astype(jnp.bfloat16)
         first, second = firsts[e], seconds[e]
         wide = second.astype(jnp.float32)
-        back_second = contract(w_out[...], impulse, 1, 0) * (1.0 - wide * wide)
+        back_second = contract(w_out[...], impulse, 0, 0) * (1.0 - wide * wide)
         back_second = back_second.astype(jnp.bfloat16)
         wide = first.astype(jnp.float32)
         back_first = contract(w_mid[...], back_second, 1, 0) * (1.0 - wide * wide)
@@ -317,65 +348,47 @@
     lax.fori_loop(0, ELEMS, backward, 0)
 
     for r in range(32):
-        pieces[r // 4, r % 4] = grads[PIECE * r : PIECE * (r + 1)]
-    sends = []
-
-    def push(source, target, send_sem, recv_sem, device):
-        copy = pltpu.make_async_remote_copy(
-            src_ref=source,
-            dst_ref=target,
-            send_sem=send_sem,
-            recv_sem=recv_sem,
-            device_id=device,
-            device_id_type=MESH,
+        pieces[r] = grads[PIECE * r : PIECE * (r + 1)]
+    arriving = [
+        push(
+            pieces.at[(rank + d) % 32],
+            plane_in.at[d - 1],
+            rs_send.at[d - 1],
+            rs_recv.at[d - 1],
+            in_plane(d),
         )
-        copy.start()
-        sends.append(copy)
-        return copy
-
-    arriving = [
-        push(pieces.at[(q + d) % 8], rs1.at[d - 1], rs1_send.at[d - 1], rs1_recv.at[d - 1], in_plane(d))
-        for d in range(1, 8)
+        for d in range(1, 32)
     ]
-    total = pieces[q]
-    for d in range(1, 8):
+    total = pieces[rank]
+    for d in range(1, 32):
         arriving[d - 1].wait_recv()
-        total = total + rs1[d - 1]
-    mine[...] = total
-    arriving = [
-        push(mine.at[(x + d) % 4], rs2.at[d - 1], rs2_send.at[d - 1], rs2_recv.at[d - 1], along_x(d))
-        for d in range(1, 4)
-    ]
-    total = mine[x]
-    for d in range(1, 4):
-        arriving[d - 1].wait_recv()
-        total = total + rs2[d - 1]
-
-    ring_a[zl] = total
-    arriving = [
-        push(ring_a.at[zl], ring_a.at[zl], a_send.at[d - 1], a_recv.at[d - 1], in_block(d))
-        for d in range(1, ZBLOCK)
-    ]
-    for copy in arriving:
-        copy.wait_recv()
-    total = ring_a[0]
-    for d in range(1, ZBLOCK):
-        total = total + ring_a[d]
+        total = total + plane_in[d - 1]
+
+    if ZBLOCK > 1:
+        ring_a[zl] = total
+        arriving = [
+            push(ring_a.at[zl], ring_a.at[zl], a_send.at[d - 1], a_recv.at[d - 1], in_block(d))
+            for d in range(1, ZBLOCK)
+        ]
+        for copy in arriving:
+            copy.wait_recv()
+        total = ring_a[0]
+        for d in range(1, ZBLOCK):
+            total = total + ring_a[d]
     ring_b[zh] = total
     pl.semaphore_wait(far_two, 2)
     across_z = [
         push(ring_b.at[zh], ring_b.at[zh], b_send.at[d - 1], b_recv.at[d - 1], across(d))
-        for d in range(1, outer)
+        for d in sorted(range(1, OUTER), key=lambda d: (-min(d, OUTER - d), d))
     ]
 
-    table_copy.wait()
+    for fetch in fetches[8:]:
+        fetch.wait()
     rows = jnp.concatenate([asm[:, e * NODES : (e + 1) * NODES] for e in range(ELEMS)], axis=0)
     high = rows.astype(jnp.bfloat16)
     low = (rows - high.astype(jnp.float32)).astype(jnp.bfloat16)
     along_one = (
-        contract(high, one_vmem[0], 1, 0)
-        + contract(low, one_vmem[0], 1, 0)
-        + contract(high, one_vmem[1], 1, 0)
+        contract(high, one[0], 1, 0) + contract(low, one[0], 1, 0) + contract(high, one[1], 1, 0)
     )
     for e in range(ELEMS):
         toward = contract(w_in[...], back_firsts[e], 1, 0)
@@ -393,58 +406,64 @@
                 + diff[1, e] * others[:, 0:LANES]
                 + diff[2, e] * others[:, LANES:]
             )
-            here = slice(e * NODES + part * LANES, e * NODES + (part + 1) * LANES)
-            value = asm[:, here] + step_scale * viscous
-            out[0, :, here] = value[0:FIELDS] + toward[:, lanes]
+            chunk = e * (NODES // LANES) + part
+            value = asm[:, chunk * LANES : (chunk + 1) * LANES] + step_scale * viscous
+            out[pl.ds(chunk, FIELDS, stride=CHUNKS), :] = value[0:FIELDS] + toward[:, lanes]
 
     for copy in across_z:
         copy.wait_recv()
     total = ring_b[0]
-    for d in range(1, outer):
+    for d in range(1, OUTER):
         total = total + ring_b[d]
 
-    final[q, x] = total
+    final[rank] = total
     arriving = [
-        push(final.at[q, x], final.at[q, x], g1_send.at[d - 1], g1_recv.at[d - 1], along_x(d))
-        for d in range(1, 4)
+        push(final.at[rank], final.at[rank], g_send.at[d - 1], g_recv.at[d - 1], in_plane(d))
+        for d in range(1, 32)
     ]
     for copy in arriving:
         copy.wait_recv()
-    arriving = [
-        push(final.at[q], final.at[q], g2_send.at[d - 1], g2_recv.at[d - 1], in_plane(d))
-        for d in range(1, 8)
-    ]
-    for copy in arriving:
-        copy.wait_recv()
+    for copy in sends:
+        copy.wait_send()
+
+
+def finish(state_in, final, state_out, gin, gmid, gout, rows, sem):
+    copy = pltpu.make_async_copy(state_in, state_out, sem)
+    copy.start()
     for r in range(32):
-        grads[PIECE * r : PIECE * (r + 1)] = final[r // 4, r % 4]
-    gmid[...] = grads[0:128]
-    gin[...] = grads[128 : 128 + FIELDS]
-    gout[...] = grads[144:160].T[:, 0:FIELDS]
-
-    for copy in halo + sends:
-        copy.wait_send()
+        rows[PIECE * r : PIECE * (r + 1)] = final[r]
+    gmid[...] = rows[0:128]
+    gin[...] = rows[128 : 128 + FIELDS]
+    gout[...] = rows[144 : 144 + FIELDS]
+    copy.wait()
 
 
 def per_device(state, cotangent, diffusivity, shared_nodes, w_in, b_in, w_mid, b_mid, w_out):
     f32, bf16 = jnp.float32, jnp.bfloat16
     one, two_three = direction_tables()
     vmem = pl.BlockSpec(memory_space=pltpu.VMEM)
+    hbm = pl.BlockSpec(memory_space=pltpu.HBM)
     dma = pltpu.SemaphoreType.DMA
-    outer = 32 // ZBLOCK
-    return pl.pallas_call(
+    result, final = pl.pallas_call(
         body,
         out_shape=(
-            jax.ShapeDtypeStruct((1, FIELDS, LOCAL), f32),
-            jax.ShapeDtypeStruct((FIELDS, HIDDEN), f32),
-            jax.ShapeDtypeStruct((HIDDEN, HIDDEN), f32),
-            jax.ShapeDtypeStruct((HIDDEN, FIELDS), f32),
+            pltpu.VMEM((FIELDS * CHUNKS, LANES), f32),
+            pltpu.VMEM((32, PIECE, LANES), f32),
         ),
-        in_specs=[vmem, vmem, pl.BlockSpec(memory_space=pltpu.SMEM)]
-        + [vmem] * 6
-        + [pl.BlockSpec(memory_space=pl.ANY), vmem],
-        out_specs=(vmem, vmem, vmem, vmem),
+        in_specs=[hbm] * 11,
+        out_specs=(vmem, vmem),
         scratch_shapes=[
+            pltpu.VMEM((FIELDS, LOCAL), bf16),
+            pltpu.VMEM((FIELDS * CHUNKS, LANES), f32),
+            pltpu.SMEM((3, ELEMS), f32),
+            pltpu.VMEM((1, 8, SLOTS), jnp.int32),
+            pltpu.VMEM((FIELDS, HIDDEN), bf16),
+            pltpu.VMEM((HIDDEN,), f32),
+            pltpu.VMEM((HIDDEN, HIDDEN), bf16),
+            pltpu.VMEM((HIDDEN,), f32),
+            pltpu.VMEM((FIELDS, HIDDEN), bf16),
+            pltpu.VMEM((2, NODES, NODES), bf16),
+            pltpu.VMEM((2, LANES, 2 * LANES), bf16),
             pltpu.VMEM((ROWS, LOCAL), f32),
             pltpu.VMEM((BLOCKS, 8, LANES), jnp.int32),
             pltpu.VMEM((BLOCKS, ROWS, LANES), f32),
@@ -459,48 +478,54 @@
             pltpu.VMEM((ELEMS, HIDDEN, NODES), bf16),
             pltpu.VMEM((ELEMS, HIDDEN, NODES), bf16),
             pltpu.VMEM((160, HIDDEN), f32),
-            pltpu.VMEM((8, 4, PIECE, LANES), f32),
-            pltpu.VMEM((7, 4, PIECE, LANES), f32),
-            pltpu.VMEM((3, PIECE, LANES), f32),
-            pltpu.VMEM((4, PIECE, LANES), f32),
+            pltpu.VMEM((32, PIECE, LANES), f32),
+            pltpu.VMEM((31, PIECE, LANES), f32),
             pltpu.VMEM((ZBLOCK, PIECE, LANES), f32),
-            pltpu.VMEM((outer, PIECE, LANES), f32),
-            pltpu.VMEM((8, 4, PIECE, LANES), f32),
-            pltpu.VMEM((2, NODES, NODES), bf16),
-            dma,
+            pltpu.VMEM((OUTER, PIECE, LANES), f32),
+            dma((11,)),
             dma((8,)),
             dma((8,)),
-            dma((7,)),
-            dma((7,)),
-            dma((3,)),
-            dma((3,)),
-            dma((ZBLOCK - 1,)),
-            dma((ZBLOCK - 1,)),
-            dma((outer - 1,)),
-            dma((outer - 1,)),
-            dma((3,)),
-            dma((3,)),
-            dma((7,)),
-            dma((7,)),
+            dma((31,)),
+            dma((31,)),
+            dma((max(ZBLOCK - 1, 1),)),
+            dma((max(ZBLOCK - 1, 1),)),
+            dma((OUTER - 1,)),
+            dma((OUTER - 1,)),
+            dma((31,)),
+            dma((31,)),
             pltpu.SemaphoreType.REGULAR,
             pltpu.SemaphoreType.REGULAR,
         ],
         compiler_params=pltpu.CompilerParams(
-            collective_id=0, has_side_effects=True, vmem_limit_bytes=32 * 1024 * 1024
+            collective_id=0, has_side_effects=True, vmem_limit_bytes=66_500_000
         ),
     )(
         state,
-        cotangent,
+        cotangent.reshape(FIELDS * CHUNKS, LANES),
         diffusivity,
         shared_nodes,
         w_in,
         b_in,
         w_mid,
         b_mid,
-        w_out,
+        w_out.T,
         jnp.asarray(one),
         jnp.asarray(two_three),
     )
+    grad_state, grad_in, grad_mid, grad_out = pl.pallas_call(
+        finish,
+        out_shape=(
+            jax.ShapeDtypeStruct((FIELDS * CHUNKS, LANES), f32),
+            jax.ShapeDtypeStruct((FIELDS, HIDDEN), f32),
+            jax.ShapeDtypeStruct((HIDDEN, HIDDEN), f32),
+            jax.ShapeDtypeStruct((FIELDS, HIDDEN), f32),
+        ),
+        in_specs=[vmem, vmem],
+        out_specs=(hbm, vmem, vmem, vmem),
+        scratch_shapes=[pltpu.VMEM((160, HIDDEN), f32), dma],
+        compiler_params=pltpu.CompilerParams(vmem_limit_bytes=8 * 1024 * 1024),
+    )(result, final)
+    return grad_state.reshape(1, FIELDS, LOCAL), grad_in, grad_mid, grad_out.T
 
 
 def solution(mesh):

time: 73.3 us -> 61.2 us (0.83)
  local copies, waits for them, and re-layouts: 6.12 us -> 0 us
  Pallas kernels: 66.2 us -> 60.4 us
    pallas_call x1 -> x2, Pallas kernels: 66.2 us -> 60.4 us  [the longest x1 59.1 us: per_device(): pl.pallas_call(body, out_shape=(pltpu.VMEM((FIELDS * CHUNKS, LANES), f32)...]
    unnamed x22 -> x0, local copies, waits for them, and re-layouts: 4.52 us -> none
    pallas_call x2 -> x0, local copies, waits for them, and re-layouts: 1.6 us -> none  [per_device(): pl.pallas_call(body, out_shape=(jax.ShapeDtypeStruct((1, FIELDS, LOCAL),...]
where the time goes in v2:
time: 61.2 us; the launch traced here: 61.1 us
  Pallas kernels  60.4 us (99%)
  between operations  0.64 us (1%)
    pallas_call x1, Pallas kernels, per_device(): pl.pallas_call(body, out_shape=(pltpu.VMEM((FIELDS * CHUNKS, LANES), f32)...  59.1 us
    pallas_call x1, Pallas kernels, per_device(): pl.pallas_call(finish, out_shape=(jax.ShapeDtypeStruct((FIELDS * CHUNKS,...  1.33 us

profile of v2, /device:TPU:1, one launch (start us, length us, event | category | flops | bytes accessed | tf_op | source)
XLA Modules:
  0.0 61.1 jit_solution(12505970848582506143)
XLA Ops:
  0.6 59.1 %shard_map.138 = (f32[448,128]{1,0:T(8,128)S(1)}, f32[32,5,128]{2,1,0:T(8,128)S(1)}) custom-call(bf16[14,4096]{1,0:T(8,128)(2,1)} %state_hbm.1, f32[448,128]{1,0:T(8,128)} %bitcast.4, f32[3,8]{1,0:T(4,128)} %diff_hbm.1, s32[1,8,384]{2,1,0:T(8,128)} %lists_hbm.1, bf16[14,128]{1,0:T(8,128)(2,1)} %w_in_hbm.1, f32[128]{0:T(128)} %b_in_hbm.1, ...), custom_call_target="tpu_custom_call" | custom-call | tf_op jit(solution)/shard_map/pallas_call | solution.py:447
  59.7 1.3 %shard_map.139 = (f32[448,128]{1,0:T(8,128)}, f32[14,128]{1,0:T(8,128)}, f32[128,128]{1,0:T(8,128)}, f32[14,128]{1,0:T(8,128)}) custom-call(f32[448,128]{1,0:T(8,128)S(1)} %get-tuple-element.10.state_in, f32[32,5,128]{2,1,0:T(8,128)S(1)} %get-tuple-element.11.final), custom_call_target="tpu_custom_call" | custom-call | tf_op jit(solution)/shard_map/pallas_call | solution.py:515

commit v3 on v2

--- a/solution.py
+++ b/solution.py
@@ -22,9 +22,12 @@
 PIECE = 5
 MESH = pl.DeviceIdType.MESH
 OFFSETS = (1, -1, PROWS, -PROWS, PROWS + 1, -PROWS - 1, PROWS - 1, -PROWS + 1)
-ZBLOCK = 1
-OUTER = 32 // ZBLOCK
-NEAR_Z = (1, 2, 3, 4, -1, -2, -3, -4)
+PLANE = sorted(
+    ((dx, dy, dc) for dx in range(4) for dy in range(4) for dc in range(2) if dx or dy or dc),
+    key=lambda step: -min(step[0], 4 - step[0]) - min(step[1], 4 - step[1]),
+)
+DEPTH = 32
+NEAR_Z = (3, -3, 2, -2, 1, -1)
 
 step_scale = 0.5
 
@@ -119,52 +122,55 @@
     asm,
     firsts,
     seconds,
+    first_slopes,
+    second_slopes,
     back_firsts,
     grads,
     pieces,
     plane_in,
-    ring_a,
-    ring_b,
+    along,
     fetched,
     halo_send,
     halo_recv,
     rs_send,
     rs_recv,
-    a_send,
-    a_recv,
-    b_send,
-    b_recv,
+    z_send,
+    z_recv,
     g_send,
     g_recv,
+    plane_here,
     far_one,
     far_two,
+    far_three,
 ):
     graph = lax.axis_index("graph")
     x = lax.axis_index("group")
-    z = graph // 8
-    q = graph % 8
+    z = lax.div(graph, 8)
+    q = lax.rem(graph, 8)
+    y = lax.div(q, 2)
+    core = lax.rem(q, 2)
     rank = x * 8 + q
-    zl = z % ZBLOCK
-    zh = z // ZBLOCK
 
     def place(z_at, q_at, x_at):
         return {"graph": z_at * 8 + q_at, "group": x_at}
 
     def beside(offset):
-        return {"graph": (graph + offset + 256) % 256, "group": x}
-
-    def in_plane(d):
-        other = (rank + d) % 32
-        return place(z, other % 8, other // 8)
-
-    def in_block(d):
-        return place(zh * ZBLOCK + (zl + d) % ZBLOCK, q, x)
-
-    def across(d):
-        return place(((zh + d) % OUTER) * ZBLOCK + zl, q, x)
+        return {"graph": lax.rem(graph + (offset + 256), 256), "group": x}
+
+    def step_place(step):
+        dx, dy, dc = step
+        q_at = lax.rem(y + dy, 4) * 2 + lax.rem(core + dc, 2)
+        return q_at, lax.rem(x + dx, 4)
+
+    def step_rank(step):
+        q_at, x_at = step_place(step)
+        return x_at * 8 + q_at
+
+    def in_plane(step):
+        return place(z, *step_place(step))
 
     def along_z(d):
-        return place((z + d + 32) % 32, q, x)
+        return place(lax.rem(z + (d + 32), 32), q, x)
 
     def signal(semaphore, target):
         pl.semaphore_signal(semaphore, inc=1, device_id=target, device_id_type=MESH)
@@ -191,9 +197,11 @@
         fetch.start()
 
     barrier = pltpu.get_barrier_semaphore()
-    near = [beside(o) for o in OFFSETS]
-    near += [along_z(d) for d in NEAR_Z]
-    near += [in_plane(d) for d in range(1, 32)]
+    along_x = [step for step in PLANE if step[1] == step[2] == 0]
+    near = [along_z(d) for d in NEAR_Z]
+    near += [beside(o) for o in OFFSETS]
+    near += [in_plane(step) for step in PLANE if step[0] == 0]
+    near += [in_plane(step) for step in along_x]
     for target in near:
         signal(barrier, target)
 
@@ -254,7 +262,7 @@
 
     pl.semaphore_wait(barrier, len(near))
     halo = []
-    for k in (2, 3, 0, 1, 4, 5, 6, 7):
+    for k in (2, 3, 4, 5, 6, 7, 0, 1):
         if k < 4:
             source = send_blocks.at[3 * k : 3 * k + 3, 0:FIELDS]
             target = face_in.at[3 * (k ^ 1) : 3 * (k ^ 1) + 3, 0:FIELDS]
@@ -262,7 +270,9 @@
             source = send_blocks.at[FACE_BLOCKS + (k - 4) // 2, 0:FIELDS]
             target = diag_in.at[(k ^ 1) - 4, 0:FIELDS]
         halo.append(push(source, target, halo_send.at[k], halo_recv.at[k ^ 1], beside(OFFSETS[k])))
-    for d in (4, -4):
+    for step in along_x:
+        signal(plane_here, in_plane(step))
+    for d in (3, -3):
         signal(far_one, along_z(d))
 
     lane_f = lane.astype(jnp.float32)
@@ -290,25 +300,24 @@
         inputs = state[:, span(e, NODES)]
         first = jnp.tanh(contract(w_in[...], inputs, 0, 0) + bias_in).astype(jnp.bfloat16)
         firsts[e] = first
+        wide = first.astype(jnp.float32)
+        first_slopes[e] = 1.0 - wide * wide
         second = jnp.tanh(contract(w_mid[...], first, 0, 0) + bias_mid).astype(jnp.bfloat16)
         seconds[e] = second
+        wide = second.astype(jnp.float32)
+        second_slopes[e] = 1.0 - wide * wide
         return carry
 
     lax.fori_loop(0, ELEMS, forward, 0)
 
     pl.semaphore_wait(far_one, 2)
-    for d in (8, -8):
+    for d in (6, -6):
         signal(far_two, along_z(d))
 
-    for copy in halo:
-        copy.wait_recv()
-
-    def assemble(h, carry):
+    def arrived(h, blocks, top, bottom):
         where_block = inv_block[h]
         where_lane = inv_lane[h]
-        top = jnp.zeros((8, LANES), jnp.float32)
-        bottom = jnp.zeros((8, LANES), jnp.float32)
-        for b in range(BLOCKS):
+        for b in blocks:
             match = where_block == b + 1
             if b < FACE_BLOCKS:
                 upper, lower = face_in[b, 0:8], face_in[b, 8:16]
@@ -318,14 +327,34 @@
                 lower = jnp.where(leading, diag_in[k + 1, 8:16], diag_in[k, 8:16])
             top = jnp.where(match, pick(upper, where_lane), top)
             bottom = jnp.where(match, pick(lower, where_lane), bottom)
-        shared = where_block > 0
+        return top, bottom
+
+    def assemble_some(h, carry):
+        zero = jnp.zeros((8, LANES), jnp.float32)
+        top, bottom = arrived(h, (0, 1, 2, 3, 4, 5, 12, 13), zero, zero)
+        asm[0:8, span(h, LANES)] = top
+        asm[8:16, span(h, LANES)] = bottom
+        return carry
+
+    def assemble(h, carry):
+        top, bottom = asm[0:8, span(h, LANES)], asm[8:16, span(h, LANES)]
+        top, bottom = arrived(h, range(6, 12), top, bottom)
+        shared = inv_block[h] > 0
         own = cot16[0:8, span(h, LANES)]
         asm[0:8, span(h, LANES)] = jnp.where(shared, 0.5 * own + 0.5 * top, own)
         own = cot16[8:16, span(h, LANES)]
         asm[8:16, span(h, LANES)] = jnp.where(shared, 0.5 * own + 0.5 * bottom, own)
         return carry
 
-    lax.fori_loop(0, CHUNKS, assemble, 0, unroll=2)
+    for copy in halo[2:]:
+        copy.wait_recv()
+    lax.fori_loop(0, CHUNKS, assemble_some, 0, unroll=2)
+    for copy in halo[:2]:
+        copy.wait_recv()
+    lax.fori_loop(0, CHUNKS, assemble, 0, unroll=4)
+    pl.semaphore_wait(far_two, 2)
+    for d in (4, -4):
+        signal(far_three, along_z(d))
 
     grads[...] = jnp.zeros_like(grads)
 
@@ -333,11 +362,9 @@
         here = span(e, NODES)
         impulse = (step_scale * asm[0:FIELDS, here]).astype(jnp.bfloat16)
         first, second = firsts[e], seconds[e]
-        wide = second.astype(jnp.float32)
-        back_second = contract(w_out[...], impulse, 0, 0) * (1.0 - wide * wide)
+        back_second = contract(w_out[...], impulse, 0, 0) * second_slopes[e]
         back_second = back_second.astype(jnp.bfloat16)
-        wide = first.astype(jnp.float32)
-        back_first = contract(w_mid[...], back_second, 1, 0) * (1.0 - wide * wide)
+        back_first = contract(w_mid[...], back_second, 1, 0) * first_slopes[e]
         back_first = back_first.astype(jnp.bfloat16)
         back_firsts[e] = back_first
         grads[0:128] += contract(first, back_second, 1, 1)
@@ -349,37 +376,21 @@
 
     for r in range(32):
         pieces[r] = grads[PIECE * r : PIECE * (r + 1)]
+    pl.semaphore_wait(plane_here, 3)
     arriving = [
-        push(
-            pieces.at[(rank + d) % 32],
-            plane_in.at[d - 1],
-            rs_send.at[d - 1],
-            rs_recv.at[d - 1],
-            in_plane(d),
-        )
-        for d in range(1, 32)
+        push(pieces.at[step_rank(step)], plane_in.at[i], rs_send.at[i], rs_recv.at[i], in_plane(step))
+        for i, step in enumerate(PLANE)
     ]
     total = pieces[rank]
-    for d in range(1, 32):
-        arriving[d - 1].wait_recv()
-        total = total + plane_in[d - 1]
-
-    if ZBLOCK > 1:
-        ring_a[zl] = total
-        arriving = [
-            push(ring_a.at[zl], ring_a.at[zl], a_send.at[d - 1], a_recv.at[d - 1], in_block(d))
-            for d in range(1, ZBLOCK)
-        ]
-        for copy in arriving:
-            copy.wait_recv()
-        total = ring_a[0]
-        for d in range(1, ZBLOCK):
-            total = total + ring_a[d]
-    ring_b[zh] = total
-    pl.semaphore_wait(far_two, 2)
+    for i, copy in enumerate(arriving):
+        copy.wait_recv()
+        total = total + plane_in[i]
+
+    along[z] = total
+    pl.semaphore_wait(far_three, 2)
     across_z = [
-        push(ring_b.at[zh], ring_b.at[zh], b_send.at[d - 1], b_recv.at[d - 1], across(d))
-        for d in sorted(range(1, OUTER), key=lambda d: (-min(d, OUTER - d), d))
+        push(along.at[z], along.at[z], z_send.at[d - 1], z_recv.at[d - 1], along_z(d))
+        for d in sorted(range(1, DEPTH), key=lambda d: (-min(d, DEPTH - d), d))
     ]
 
     for fetch in fetches[8:]:
@@ -410,16 +421,19 @@
             value = asm[:, chunk * LANES : (chunk + 1) * LANES] + step_scale * viscous
             out[pl.ds(chunk, FIELDS, stride=CHUNKS), :] = value[0:FIELDS] + toward[:, lanes]
 
-    for copy in across_z:
+    for copy in sends:
+        copy.wait_send()
+    sends.clear()
+    for copy in reversed(across_z):
         copy.wait_recv()
-    total = ring_b[0]
-    for d in range(1, OUTER):
-        total = total + ring_b[d]
+    total = along[0]
+    for d in range(1, DEPTH):
+        total = total + along[d]
 
     final[rank] = total
     arriving = [
-        push(final.at[rank], final.at[rank], g_send.at[d - 1], g_recv.at[d - 1], in_plane(d))
-        for d in range(1, 32)
+        push(final.at[rank], final.at[rank], g_send.at[i], g_recv.at[i], in_plane(step))
+        for i, step in enumerate(PLANE)
     ]
     for copy in arriving:
         copy.wait_recv()
@@ -476,23 +490,24 @@
             pltpu.VMEM((ROWS, LOCAL), f32),
             pltpu.VMEM((ELEMS, HIDDEN, NODES), bf16),
             pltpu.VMEM((ELEMS, HIDDEN, NODES), bf16),
+            pltpu.VMEM((ELEMS, HIDDEN, NODES), f32),
+            pltpu.VMEM((ELEMS, HIDDEN, NODES), f32),
             pltpu.VMEM((ELEMS, HIDDEN, NODES), bf16),
             pltpu.VMEM((160, HIDDEN), f32),
             pltpu.VMEM((32, PIECE, LANES), f32),
             pltpu.VMEM((31, PIECE, LANES), f32),
-            pltpu.VMEM((ZBLOCK, PIECE, LANES), f32),
-            pltpu.VMEM((OUTER, PIECE, LANES), f32),
+            pltpu.VMEM((DEPTH, PIECE, LANES), f32),
             dma((11,)),
             dma((8,)),
             dma((8,)),
             dma((31,)),
             dma((31,)),
-            dma((max(ZBLOCK - 1, 1),)),
-            dma((max(ZBLOCK - 1, 1),)),
-            dma((OUTER - 1,)),
-            dma((OUTER - 1,)),
+            dma((DEPTH - 1,)),
+            dma((DEPTH - 1,)),
             dma((31,)),
             dma((31,)),
+            pltpu.SemaphoreType.REGULAR,
+            pltpu.SemaphoreType.REGULAR,
             pltpu.SemaphoreType.REGULAR,
             pltpu.SemaphoreType.REGULAR,
         ],

time: 61.2 us -> 62.9 us (1.028)
  Pallas kernels: 60.4 us -> 62.1 us
    pallas_call x1, Pallas kernels: 59.1 us -> 60.8 us  [per_device(): pl.pallas_call(body, out_shape=(pltpu.VMEM((FIELDS * CHUNKS, LANES), f32)...]
where the time goes in v3:
time: 62.9 us; the launch traced here: 62.7 us
  Pallas kernels  62.1 us (99%)
  between operations  0.64 us (1%)
    pallas_call x1, Pallas kernels, per_device(): pl.pallas_call(body, out_shape=(pltpu.VMEM((FIELDS * CHUNKS, LANES), f32)...  60.8 us
    pallas_call x1, Pallas kernels, per_device(): pl.pallas_call(finish, out_shape=(jax.ShapeDtypeStruct((FIELDS * CHUNKS,...  1.33 us

profile of v3, /device:TPU:1, one launch (start us, length us, event | category | flops | bytes accessed | tf_op | source)
XLA Modules:
  0.0 62.7 jit_solution(5486211182607728056)
XLA Ops:
  0.6 60.8 %shard_map.138 = (f32[448,128]{1,0:T(8,128)S(1)}, f32[32,5,128]{2,1,0:T(8,128)S(1)}) custom-call(bf16[14,4096]{1,0:T(8,128)(2,1)} %state_hbm.1, f32[448,128]{1,0:T(8,128)} %bitcast.4, f32[3,8]{1,0:T(4,128)} %diff_hbm.1, s32[1,8,384]{2,1,0:T(8,128)} %lists_hbm.1, bf16[14,128]{1,0:T(8,128)(2,1)} %w_in_hbm.1, f32[128]{0:T(128)} %b_in_hbm.1, ...), custom_call_target="tpu_custom_call" | custom-call | tf_op jit(solution)/shard_map/pallas_call | solution.py:461
  61.4 1.3 %shard_map.139 = (f32[448,128]{1,0:T(8,128)}, f32[14,128]{1,0:T(8,128)}, f32[128,128]{1,0:T(8,128)}, f32[14,128]{1,0:T(8,128)}) custom-call(f32[448,128]{1,0:T(8,128)S(1)} %get-tuple-element.10.state_in, f32[32,5,128]{2,1,0:T(8,128)S(1)} %get-tuple-element.11.final), custom_call_target="tpu_custom_call" | custom-call | tf_op jit(solution)/shard_map/pallas_call | solution.py:530

commit v4 on v3

--- a/solution.py
+++ b/solution.py
@@ -27,7 +27,7 @@
     key=lambda step: -min(step[0], 4 - step[0]) - min(step[1], 4 - step[1]),
 )
 DEPTH = 32
-NEAR_Z = (3, -3, 2, -2, 1, -1)
+NEAR_Z = (4, -4, 3, -3, 2, -2, 1, -1)
 
 step_scale = 0.5
 
@@ -138,10 +138,8 @@
     z_recv,
     g_send,
     g_recv,
-    plane_here,
     far_one,
     far_two,
-    far_three,
 ):
     graph = lax.axis_index("graph")
     x = lax.axis_index("group")
@@ -197,11 +195,9 @@
         fetch.start()
 
     barrier = pltpu.get_barrier_semaphore()
-    along_x = [step for step in PLANE if step[1] == step[2] == 0]
     near = [along_z(d) for d in NEAR_Z]
     near += [beside(o) for o in OFFSETS]
-    near += [in_plane(step) for step in PLANE if step[0] == 0]
-    near += [in_plane(step) for step in along_x]
+    near += [in_plane(step) for step in PLANE]
     for target in near:
         signal(barrier, target)
 
@@ -262,7 +258,7 @@
 
     pl.semaphore_wait(barrier, len(near))
     halo = []
-    for k in (2, 3, 4, 5, 6, 7, 0, 1):
+    for k in (2, 3, 0, 1, 4, 5, 6, 7):
         if k < 4:
             source = send_blocks.at[3 * k : 3 * k + 3, 0:FIELDS]
             target = face_in.at[3 * (k ^ 1) : 3 * (k ^ 1) + 3, 0:FIELDS]
@@ -270,9 +266,7 @@
             source = send_blocks.at[FACE_BLOCKS + (k - 4) // 2, 0:FIELDS]
             target = diag_in.at[(k ^ 1) - 4, 0:FIELDS]
         halo.append(push(source, target, halo_send.at[k], halo_recv.at[k ^ 1], beside(OFFSETS[k])))
-    for step in along_x:
-        signal(plane_here, in_plane(step))
-    for d in (3, -3):
+    for d in (4, -4):
         signal(far_one, along_z(d))
 
     lane_f = lane.astype(jnp.float32)
@@ -311,7 +305,7 @@
     lax.fori_loop(0, ELEMS, forward, 0)
 
     pl.semaphore_wait(far_one, 2)
-    for d in (6, -6):
+    for d in (8, -8):
         signal(far_two, along_z(d))
 
     def arrived(h, blocks, top, bottom):
@@ -329,16 +323,9 @@
             bottom = jnp.where(match, pick(lower, where_lane), bottom)
         return top, bottom
 
-    def assemble_some(h, carry):
+    def assemble(h, carry):
         zero = jnp.zeros((8, LANES), jnp.float32)
-        top, bottom = arrived(h, (0, 1, 2, 3, 4, 5, 12, 13), zero, zero)
-        asm[0:8, span(h, LANES)] = top
-        asm[8:16, span(h, LANES)] = bottom
-        return carry
-
-    def assemble(h, carry):
-        top, bottom = asm[0:8, span(h, LANES)], asm[8:16, span(h, LANES)]
-        top, bottom = arrived(h, range(6, 12), top, bottom)
+        top, bottom = arrived(h, range(BLOCKS), zero, zero)
         shared = inv_block[h] > 0
         own = cot16[0:8, span(h, LANES)]
         asm[0:8, span(h, LANES)] = jnp.where(shared, 0.5 * own + 0.5 * top, own)
@@ -346,21 +333,19 @@
         asm[8:16, span(h, LANES)] = jnp.where(shared, 0.5 * own + 0.5 * bottom, own)
         return carry
 
-    for copy in halo[2:]:
+    for copy in halo:
         copy.wait_recv()
-    lax.fori_loop(0, CHUNKS, assemble_some, 0, unroll=2)
-    for copy in halo[:2]:
-        copy.wait_recv()
-    lax.fori_loop(0, CHUNKS, assemble, 0, unroll=4)
-    pl.semaphore_wait(far_two, 2)
-    for d in (4, -4):
-        signal(far_three, along_z(d))
-
     grads[...] = jnp.zeros_like(grads)
 
-    def backward(e, carry):
+    def assemble_element(e):
+        for part in range(NODES // LANES):
+            assemble(e * (NODES // LANES) + part, 0)
+
+    def backward(e, ahead):
         here = span(e, NODES)
         impulse = (step_scale * asm[0:FIELDS, here]).astype(jnp.bfloat16)
+        if ahead:
+            assemble_element(e + 1)
         first, second = firsts[e], seconds[e]
         back_second = contract(w_out[...], impulse, 0, 0) * second_slopes[e]
         back_second = back_second.astype(jnp.bfloat16)
@@ -370,13 +355,17 @@
         grads[0:128] += contract(first, back_second, 1, 1)
         grads[128 : 128 + FIELDS] += contract(state[:, here], back_first, 1, 1)
         grads[144 : 144 + FIELDS] += contract(impulse, second, 1, 1)
+
+    def backward_ahead(e, carry):
+        backward(e, True)
         return carry
 
-    lax.fori_loop(0, ELEMS, backward, 0)
+    assemble_element(0)
+    lax.fori_loop(0, ELEMS - 1, backward_ahead, 0)
+    backward(ELEMS - 1, False)
 
     for r in range(32):
         pieces[r] = grads[PIECE * r : PIECE * (r + 1)]
-    pl.semaphore_wait(plane_here, 3)
     arriving = [
         push(pieces.at[step_rank(step)], plane_in.at[i], rs_send.at[i], rs_recv.at[i], in_plane(step))
         for i, step in enumerate(PLANE)
@@ -387,7 +376,7 @@
         total = total + plane_in[i]
 
     along[z] = total
-    pl.semaphore_wait(far_three, 2)
+    pl.semaphore_wait(far_two, 2)
     across_z = [
         push(along.at[z], along.at[z], z_send.at[d - 1], z_recv.at[d - 1], along_z(d))
         for d in sorted(range(1, DEPTH), key=lambda d: (-min(d, DEPTH - d), d))
@@ -508,8 +497,6 @@
             dma((31,)),
             pltpu.SemaphoreType.REGULAR,
             pltpu.SemaphoreType.REGULAR,
-            pltpu.SemaphoreType.REGULAR,
-            pltpu.SemaphoreType.REGULAR,
         ],
         compiler_params=pltpu.CompilerParams(
             collective_id=0, has_side_effects=True, vmem_limit_bytes=66_500_000

time: 62.9 us -> 58.4 us (0.928)
  Pallas kernels: 62.1 us -> 57.6 us
    pallas_call x1, Pallas kernels: 60.8 us -> 56.3 us  [per_device(): pl.pallas_call(body, out_shape=(pltpu.VMEM((FIELDS * CHUNKS, LANES), f32)...]
where the time goes in v4:
time: 58.4 us; the launch traced here: 58.3 us
  Pallas kernels  57.6 us (99%)
  between operations  0.64 us (1%)
    pallas_call x1, Pallas kernels, per_device(): pl.pallas_call(body, out_shape=(pltpu.VMEM((FIELDS * CHUNKS, LANES), f32)...  56.3 us
    pallas_call x1, Pallas kernels, per_device(): pl.pallas_call(finish, out_shape=(jax.ShapeDtypeStruct((FIELDS * CHUNKS,...  1.33 us

profile of v4, /device:TPU:1, one launch (start us, length us, event | category | flops | bytes accessed | tf_op | source)
XLA Modules:
  0.0 58.3 jit_solution(9060391718058814465)
XLA Ops:
  0.6 56.3 %shard_map.138 = (f32[448,128]{1,0:T(8,128)S(1)}, f32[32,5,128]{2,1,0:T(8,128)S(1)}) custom-call(bf16[14,4096]{1,0:T(8,128)(2,1)} %state_hbm.1, f32[448,128]{1,0:T(8,128)} %bitcast.4, f32[3,8]{1,0:T(4,128)} %diff_hbm.1, s32[1,8,384]{2,1,0:T(8,128)} %lists_hbm.1, bf16[14,128]{1,0:T(8,128)(2,1)} %w_in_hbm.1, f32[128]{0:T(128)} %b_in_hbm.1, ...), custom_call_target="tpu_custom_call" | custom-call | tf_op jit(solution)/shard_map/pallas_call | solution.py:450
  57.0 1.3 %shard_map.139 = (f32[448,128]{1,0:T(8,128)}, f32[14,128]{1,0:T(8,128)}, f32[128,128]{1,0:T(8,128)}, f32[14,128]{1,0:T(8,128)}) custom-call(f32[448,128]{1,0:T(8,128)S(1)} %get-tuple-element.10.state_in, f32[32,5,128]{2,1,0:T(8,128)S(1)} %get-tuple-element.11.final), custom_call_target="tpu_custom_call" | custom-call | tf_op jit(solution)/shard_map/pallas_call | solution.py:517
